TPU v7x, 32 devices: a whole 2x2x4 slice. The times are simulated.
32 devices in a mesh: grp: 4 (over z), seq: 8 (over y, x, core).
Axes of the slice: x: 2, y: 2, z: 4, core: 2. Of those that a mesh axis runs over, the one named last changes fastest.
Arguments:
- fine_rows: bfloat16 [4, 1024, 2048], P('grp', 'seq'), may hold values from -6 to 6
- segment_ids: int32 [4, 1024], P('grp', 'seq'), may hold values from 0 to 7, as said below
- pool_gain: float32 [2048], replicated, may hold values from 0.1 to 1.9
- w_in: bfloat16 [2048, 8192], P('grp', 'seq'), may hold values from -0.125 to 0.125
- w_gate: bfloat16 [8192, 16384], P('grp', 'seq'), may hold values from -0.0625 to 0.0625
- w_up: bfloat16 [8192, 16384], P('grp', 'seq'), may hold values from -0.0625 to 0.0625
- w_down: bfloat16 [16384, 8192], P('seq', 'grp'), may hold values from -0.046875 to 0.046875
- out_grad: bfloat16 [4, 64, 8192], P('grp'), may hold values from -6 to 6
Outputs:
- coarse_out: bfloat16 [4, 64, 8192], P('grp', None, 'seq')
- fine_grad: bfloat16 [4, 1024, 2048], P('grp', 'seq')
Inputs may be any that keep to these rules, and one draw needn't show every extreme that they name: `segment_ids`: within each shard of 128 consecutive bytes the numbers count the shard's segments from 0 upward, never falling, every segment one byte or more; a shard holds 4 to 8 segments, some shard of every document exactly 8, and every document 48 segments in all.
All inputs are finite; a program needn't handle non-finite values.
Results may differ from a plain program's by a relative error of at most 0.02.
Values may be sent and summed in bfloat16 or wider, within the bound.
A program may use at most 192 MiB of HBM per device.

v0:
```python
import jax
import jax.numpy as jnp
from jax import lax
from jax.sharding import PartitionSpec as P

SEG_CAP = 8
norm_eps = 1e-06
bf16 = jnp.bfloat16
f32 = jnp.float32


def silu_parts(gate_value):
    sigma = jax.nn.sigmoid(gate_value)
    return (gate_value * sigma, sigma * (1.0 + gate_value * (1.0 - sigma)))


def matmul(a, b):
    return jnp.dot(a, b, preferred_element_type=f32)


def matmul_t(a, b):
    return lax.dot_general(a, b, (((1,), (1,)), ((), ())), preferred_element_type=f32)


def swap_pairs(grps, seqs):
    halves = seqs // grps
    return [
        (g * seqs + p * halves + h, p * seqs + g * halves + h)
        for g in range(grps)
        for p in range(grps)
        for h in range(halves)
    ]


def grp_total(partial_value):
    return lax.psum_scatter(
        partial_value.astype(bf16), "grp", scatter_dimension=0, tiled=True
    ).astype(f32)


def make_shards(grps, seqs):
    halves = seqs // grps
    pairs = swap_pairs(grps, seqs)

    def swap(value):
        return lax.ppermute(value, ("grp", "seq"), pairs)

    def shards(fine_rows, segment_ids, pool_gain, w_in, w_gate, w_up, w_down, out_grad):
        rows_here = fine_rows[0]
        index_here = segment_ids[0]
        feat, width = w_in.shape
        slots = jnp.arange(SEG_CAP, dtype=jnp.int32)
        member = index_here[None, :] == slots[:, None]
        segment_sums = matmul(member.astype(bf16), rows_here)
        inv_rms = lax.rsqrt(jnp.mean(segment_sums * segment_sums, axis=1, keepdims=True) + norm_eps)
        pooled = (segment_sums * inv_rms * pool_gain).astype(bf16)
        live_count = jnp.max(index_here) + 1
        packed = jnp.concatenate(
            [pooled, jnp.full((1, pooled.shape[1]), live_count.astype(bf16))], axis=0
        )
        gathered = lax.all_gather(packed, "seq", axis=0)
        shard_counts = gathered[:, SEG_CAP, 0].astype(jnp.int32)
        gathered = gathered[:, :SEG_CAP].reshape(seqs * SEG_CAP, -1)
        offsets = jnp.cumsum(shard_counts) - shard_counts
        slot_count = seqs * SEG_CAP
        within = jnp.tile(slots, seqs)
        target = jnp.repeat(offsets, SEG_CAP) + within
        is_live = within < jnp.repeat(shard_counts, SEG_CAP)
        rows = slot_count * 3 // 4
        select = (target[None, :] == jnp.arange(rows, dtype=jnp.int32)[:, None]) & is_live[None, :]
        selector = select.astype(bf16)
        work_in = matmul(selector, gathered).astype(bf16)
        work_in = lax.all_to_all(
            work_in.reshape(rows, grps, feat), "grp", split_axis=1, concat_axis=0
        ).reshape(grps * rows, feat)
        x_cols = grp_total(matmul(work_in, w_in)).astype(bf16)
        seq_at = lax.axis_index("seq")
        block = w_gate.shape[0]
        piece = block // seqs
        grad_here = out_grad[0].reshape(slot_count, grps, seqs, piece)
        grad_part = lax.dynamic_index_in_dim(grad_here, seq_at, 2, keepdims=False)
        grad_part = matmul(selector, grad_part.reshape(slot_count, grps * piece)).astype(bf16)
        grad_part = lax.all_to_all(
            grad_part.reshape(rows, grps, piece), "grp", split_axis=1, concat_axis=0
        ).reshape(grps * rows, piece)
        work_grad = lax.all_gather(grad_part, "seq", axis=1, tiled=True)
        grad_hidden = grp_total(matmul_t(work_grad, w_down))

        def spread(cols):
            every = lax.all_gather(swap(cols), "seq", axis=0)
            every = every.reshape(grps, halves, rows, width)
            return every.transpose(0, 2, 1, 3).reshape(grps * rows, halves * width)

        def column_total(part):
            part = part.astype(bf16).reshape(grps, rows, halves, width)
            part = part.transpose(0, 2, 1, 3).reshape(seqs * rows, width)
            return swap(lax.psum_scatter(part, "seq", scatter_dimension=0, tiled=True)).astype(f32)

        coarse_x = spread(x_cols)
        gate_value = grp_total(matmul(coarse_x, w_gate))
        up_value = grp_total(matmul(coarse_x, w_up))
        activated, derivative = silu_parts(gate_value)
        hidden = (activated * up_value).astype(bf16)
        grad_gate = (grad_hidden * up_value * derivative).astype(bf16)
        grad_up = (grad_hidden * activated).astype(bf16)
        grad_gate = lax.all_gather(grad_gate, "grp", axis=0, tiled=True)
        grad_up = lax.all_gather(grad_up, "grp", axis=0, tiled=True)
        hidden = lax.all_gather(hidden, "grp", axis=0, tiled=True)
        back_cols = column_total(matmul_t(grad_gate, w_gate) + matmul_t(grad_up, w_up))
        down_cols = column_total(matmul(hidden, w_down))
        out_cols = (x_cols.astype(f32) + down_cols).astype(bf16)
        out_cols = matmul(selector.T, out_cols).astype(bf16)
        grad_cols = lax.dynamic_slice_in_dim(out_grad[0], seq_at * width, width, 1)
        grad_cols = matmul(selector, grad_cols)
        grad_x = (back_cols + grad_cols).astype(bf16)
        grad_x = lax.all_gather(grad_x, "grp", axis=0, tiled=True)
        term = matmul_t(grad_x, w_in).astype(bf16)
        term = lax.all_to_all(
            term.reshape(grps, rows, feat), "grp", split_axis=0, concat_axis=1
        ).reshape(rows, grps * feat)
        term = matmul(selector.T, term).astype(bf16)
        grad_pooled = lax.psum_scatter(term, "seq", scatter_dimension=0, tiled=True).astype(f32)
        weighted = grad_pooled * pool_gain
        inner = jnp.mean(weighted * segment_sums, axis=1, keepdims=True)
        grad_sums = inv_rms * weighted - segment_sums * (inv_rms * inv_rms * inv_rms) * inner
        fine_grad = matmul(member.astype(bf16).T, grad_sums.astype(bf16)).astype(bf16)
        return (out_cols[None], fine_grad[None])

    return shards


def solution(mesh):
    return jax.shard_map(
        make_shards(mesh.shape["grp"], mesh.shape["seq"]),
        mesh=mesh,
        in_specs=(
            P("grp", "seq", None),
            P("grp", "seq"),
            P(),
            P("grp", "seq"),
            P("grp", "seq"),
            P("grp", "seq"),
            P("seq", "grp"),
            P("grp", None, None),
        ),
        out_specs=(P("grp", None, "seq"), P("grp", "seq", None)),
        check_vma=False,
    )
```

profile of v0, /device:TPU:0, one launch (start us, length us, event | category | flops | bytes accessed | tf_op | source)
XLA Modules:
  0.0 326.0 jit_solution(11023302746642176019)
XLA Ops:
  7.2 1.4 multiply_reduce_fusion.1
  8.6 1.3 reduce_max.9
  10.6 0.8 multiply_convert_fusion
  11.4 11.3 %all-gather.2 = bf16[8,9,2048]{2,1,0:T(8,128)(2,1)S(1)} all-gather(bf16[1,9,2048]{2,1,0:T(8,128)(2,1)S(1)} %pad_bitcast_fusion), channel_id=2, replica_groups=mesh['grp'=4,'seq'=8] {'seq'}, dimensions={0}, use_global_device_ids=true | all-gather | bytes 331776 | tf_op jit(solution)/shard_map/all_gather | solution.py:61
  22.7 0.2 fusion.39
  22.9 0.1 iota_compare_fusion.1
  23.0 0.2 reduce-window.9
  23.2 0.1 iota_add_fusion
  23.3 0.1 add.65
  23.4 0.1 lt.18
  23.4 0.2 convolution_convert_fusion.6
  23.6 0.1 broadcast_in_dim_reshape.9
  23.8 0.7 copy.18
  24.5 4.9 %all-to-all-start = ((bf16[1,48,4,512]{3,1,0,2:T(8,128)(2,1)}), bf16[1,48,4,512]{3,1,0,2:T(8,128)(2,1)S(1)}, u32[]{:S(2)}, u32[]{:S(2)}) async-start(bf16[1,48,4,512]{3,1,0,2:T(8,128)(2,1)} %copy.18), calls=%async_computation | async-start | bytes 393216 | tf_op jit(solution)/shard_map/all_to_all | solution.py:73
  29.4 1.5 copy.28
  30.9 0.8 dynamic-slice_reduce_fusion
  31.7 0.2 convolution_convert_fusion.10
  31.9 0.1 broadcast_in_dim_reshape.10
  31.9 0.7 copy.22
  32.6 4.8 %all-to-all-done = bf16[1,48,4,512]{3,1,0,2:T(8,128)(2,1)S(1)} async-done(((bf16[1,48,4,512]{3,1,0,2:T(8,128)(2,1)}), bf16[1,48,4,512]{3,1,0,2:T(8,128)(2,1)S(1)}, u32[]{:S(2)}, u32[]{:S(2)}) %all-to-all-start) | async-done | bytes 196640 | tf_op jit(solution)/shard_map/all_to_all | solution.py:73
  37.4 3.3 %all-to-all-start.1 = ((bf16[1,48,4,256]{3,1,0,2:T(8,128)(2,1)}), bf16[1,48,4,256]{3,1,0,2:T(8,128)(2,1)S(1)}, u32[]{:S(2)}, u32[]{:S(2)}) async-start(bf16[1,48,4,256]{3,1,0,2:T(8,128)(2,1)} %copy.22), calls=%async_computation.5 | async-start | bytes 196608 | tf_op jit(solution)/shard_map/all_to_all | solution.py:83
  40.7 0.0 reduce-scatter.8.cloned.1.call-start
  40.7 1.1 convolution_convert_fusion.7
  41.9 0.0 reduce-scatter.16.cloned.1.call-start
  41.9 4.5 %all-to-all-done.1 = bf16[1,48,4,256]{3,1,0,2:T(8,128)(2,1)S(1)} async-done(((bf16[1,48,4,256]{3,1,0,2:T(8,128)(2,1)}), bf16[1,48,4,256]{3,1,0,2:T(8,128)(2,1)S(1)}, u32[]{:S(2)}, u32[]{:S(2)}) %all-to-all-start.1) | async-done | bytes 98336 | tf_op jit(solution)/shard_map/all_to_all | solution.py:83
  46.5 11.9 %all_gather.32 = bf16[192,2048]{1,0:T(8,128)(2,1)S(1)} all-gather(bf16[192,256]{1,0:T(8,128)(2,1)S(1)} %bitcast.93), channel_id=1, replica_groups=mesh['grp'=4,'seq'=8] {'seq'}, dimensions={1}, use_global_device_ids=true | all-gather | bytes 884736 | tf_op jit(solution)/shard_map/all_gather | solution.py:86
  58.4 7.2 %convolution_convert_fusion = bf16[192,2048]{1,0:T(8,128)(2,1)} fusion(bf16[192,2048]{1,0:T(8,128)(2,1)S(1)} %all_gather.32, bf16[2048,2048]{1,0:T(8,128)(2,1)} %param.14), kind=kOutput, calls=%fused_computation.1 | convolution fusion | flops 1611005952 | bytes 9961472 | tf_op jit(solution)/shard_map/dot_general | solution.py:22
  65.7 1.6 collective-permute-start
  67.3 27.1 %all-gather.1 = bf16[384,1024]{1,0:T(8,128)(2,1)S(1)} all-gather(bf16[48,1024]{1,0:T(8,128)(2,1)S(1)} %collective-permute-done), channel_id=3, replica_groups=mesh['grp'=4,'seq'=8] {'seq'}, dimensions={0}, use_global_device_ids=true | all-gather | bytes 884736 | tf_op jit(solution)/shard_map/all_gather | solution.py:90
  94.4 0.8 copy.19
  95.3 0.2 copy.27
  95.5 6.1 %convolution_convert_fusion.3 = bf16[192,2048]{1,0:T(8,128)(2,1)} fusion(bf16[192,2048]{1,0:T(8,128)(2,1)S(1)} %bitcast.87, bf16[2048,2048]{1,0:T(8,128)(2,1)} %param.12), kind=kOutput, calls=%fused_computation.4 | convolution fusion | flops 1611005952 | bytes 9961472 | tf_op jit(solution)/shard_map/dot_general | solution.py:18
  101.6 0.0 reduce-scatter.12.cloned.1.call-start
  101.6 6.1 %convolution_convert_fusion.2 = bf16[192,2048]{1,0:T(8,128)(2,1)} fusion(bf16[192,2048]{1,0:T(8,128)(2,1)S(1)} %bitcast.88, bf16[2048,2048]{1,0:T(8,128)(2,1)} %param.13), kind=kOutput, calls=%fused_computation.3 | convolution fusion | flops 1611005952 | bytes 9961472 | tf_op jit(solution)/shard_map/dot_general | solution.py:18
  107.7 0.0 reduce-scatter.18.cloned.1.call-start
  107.8 14.5 %reduce-scatter.10.cloned.1.call-done = bf16[48,2048]{1,0:T(8,128)(2,1)} async-done(((bf16[192,2048]{1,0:T(8,128)(2,1)}), bf16[48,2048]{1,0:T(8,128)(2,1)}) %reduce-scatter.10.cloned.1.call-update) | async-done | bytes 196624 | tf_op jit(solution)/shard_map/reduce_scatter | solution.py:36
  122.3 24.9 %reduce-scatter.12.cloned.1.call-done = bf16[48,2048]{1,0:T(8,128)(2,1)} async-done(((bf16[192,2048]{1,0:T(8,128)(2,1)}), bf16[48,2048]{1,0:T(8,128)(2,1)}) %reduce-scatter.12.cloned.1.call-update) | async-done | bytes 196624 | tf_op jit(solution)/shard_map/reduce_scatter | solution.py:36
  147.1 1.4 fusion.8
  148.5 18.2 %all_gather.33 = bf16[192,2048]{1,0:T(8,128)(2,1)S(1)} all-gather(bf16[48,2048]{1,0:T(8,128)(2,1)S(1)} %get-tuple-element.3), channel_id=1, replica_groups=mesh['grp'=4,'seq'=8] {'grp'}, dimensions={0}, use_global_device_ids=true | all-gather | bytes 983040 | tf_op jit(solution)/shard_map/all_gather | solution.py:106
  166.7 6.3 %fusion.43 = f32[192,2048]{1,0:T(8,128)S(1)} fusion(bf16[192,2048]{1,0:T(8,128)(2,1)S(1)} %all_gather.33, bf16[2048,2048]{1,0:T(8,128)(2,1)} %param.12), kind=kOutput, calls=%fused_computation.73 | convolution fusion | flops 1610612736 | bytes 10747904 | tf_op jit(solution)/shard_map/dot_general | solution.py:22
  173.0 17.4 %all_gather.34 = bf16[192,2048]{1,0:T(8,128)(2,1)S(1)} all-gather(bf16[48,2048]{1,0:T(8,128)(2,1)S(1)} %get-tuple-element.2), channel_id=1, replica_groups=mesh['grp'=4,'seq'=8] {'grp'}, dimensions={0}, use_global_device_ids=true | all-gather | bytes 983040 | tf_op jit(solution)/shard_map/all_gather | solution.py:107
  190.4 6.3 %fusion = bf16[192,2048]{1,0:T(8,128)(2,1)S(1)} fusion(f32[192,2048]{1,0:T(8,128)S(1)} %fusion.43, bf16[192,2048]{1,0:T(8,128)(2,1)S(1)} %all_gather.34, bf16[2048,2048]{1,0:T(8,128)(2,1)} %param.13), kind=kOutput, calls=%fused_computation.5 | convolution fusion | flops 1611399168 | bytes 11534336 | tf_op jit(solution)/shard_map/dot_general | solution.py:22
  196.7 0.6 reshape.115
  197.2 1.1 copy.23
  198.4 0.0 reduce-scatter.14.cloned.1.call-start
  198.4 16.8 %all_gather.31 = bf16[192,2048]{1,0:T(8,128)(2,1)S(1)} all-gather(bf16[48,2048]{1,0:T(8,128)(2,1)S(1)} %get-tuple-element.4), channel_id=1, replica_groups=mesh['grp'=4,'seq'=8] {'grp'}, dimensions={0}, use_global_device_ids=true | all-gather | bytes 983040 | tf_op jit(solution)/shard_map/all_gather | solution.py:108
  215.2 18.1 %reduce-scatter.18.cloned.1.call-done = bf16[48,1024]{1,0:T(8,128)(2,1)} async-done(((bf16[384,1024]{1,0:T(8,128)(2,1)}), bf16[48,1024]{1,0:T(8,128)(2,1)}) %reduce-scatter.18.cloned.1.call-update) | async-done | bytes 98320 | tf_op jit(solution)/shard_map/reduce_scatter | solution.py:97
  233.4 1.5 collective-permute-start.2
  234.9 5.2 %convolution_convert_fusion.1 = bf16[192,2048]{1,0:T(8,128)(2,1)S(1)} fusion(bf16[192,2048]{1,0:T(8,128)(2,1)S(1)} %all_gather.31, bf16[2048,2048]{1,0:T(8,128)(2,1)} %param.14), kind=kOutput, calls=%fused_computation.2 | convolution fusion | flops 1611005952 | bytes 9961472 | tf_op jit(solution)/shard_map/dot_general | solution.py:18
  240.1 0.6 reshape.112
  240.7 1.1 copy.20
  241.8 0.0 reduce-scatter.20.cloned.1.call-start
  241.9 1.1 add_convert_fusion
  243.0 16.2 %all_gather.35 = bf16[192,1024]{1,0:T(8,128)(2,1)S(1)} all-gather(bf16[48,1024]{1,0:T(8,128)(2,1)S(1)} %add_convert_fusion), channel_id=1, replica_groups=mesh['grp'=4,'seq'=8] {'grp'}, dimensions={0}, use_global_device_ids=true | all-gather | bytes 491520 | tf_op jit(solution)/shard_map/all_gather | solution.py:116
  259.1 0.5 convolution_convert_fusion.8
  259.6 11.9 %all_to_all.45 = bf16[4,48,1,512]{3,1,2,0:T(8,128)(2,1)S(1)} all-to-all(bf16[4,48,1,512]{3,1,2,0:T(8,128)(2,1)S(1)} %bitcast.85), channel_id=1, replica_groups=mesh['grp'=4,'seq'=8] {'grp'}, dimensions={0} | all-to-all | bytes 393216 | tf_op jit(solution)/shard_map/all_to_all | solution.py:118
  271.5 0.2 copy.25
  271.7 1.0 convolution_convert_fusion.5
  272.7 6.1 %reduce-scatter.14.cloned.1.call-done = bf16[48,1024]{1,0:T(8,128)(2,1)} async-done(((bf16[384,1024]{1,0:T(8,128)(2,1)}), bf16[48,1024]{1,0:T(8,128)(2,1)}) %reduce-scatter.14.cloned.1.call-update) | async-done | bytes 98320 | tf_op jit(solution)/shard_map/reduce_scatter | solution.py:97
  278.8 1.5 collective-permute-start.1
  280.3 0.9 fusion.2
  281.2 35.1 %reduce-scatter.20.cloned.1.call-done = bf16[8,2048]{1,0:T(8,128)(2,1)} async-done(((bf16[64,2048]{1,0:T(8,128)(2,1)}), bf16[8,2048]{1,0:T(8,128)(2,1)}) %reduce-scatter.20.cloned.1.call-update) | async-done | bytes 32784 | tf_op jit(solution)/shard_map/reduce_scatter | solution.py:122
  316.3 0.9 multiply_reduce_fusion
  317.2 1.9 fusion.1
  (27 shorter events, 0.3 us)
Async XLA Ops:
  7.2 33.6 %copy-start = (bf16[512,1024]{1,0:T(8,128)(2,1)S(1)}, bf16[512,1024]{1,0:T(8,128)(2,1)}, u32[]{:S(2)}) copy-start(bf16[512,1024]{1,0:T(8,128)(2,1)} %param.11) | copy-start | bytes 3145732
  24.5 12.9 %all-to-all-start = ((bf16[1,48,4,512]{3,1,0,2:T(8,128)(2,1)}), bf16[1,48,4,512]{3,1,0,2:T(8,128)(2,1)S(1)}, u32[]{:S(2)}, u32[]{:S(2)}) async-start(bf16[1,48,4,512]{3,1,0,2:T(8,128)(2,1)} %copy.18), calls=%async_computation | async-start | bytes 393216 | tf_op jit(solution)/shard_map/all_to_all | solution.py:73
  37.4 9.1 %all-to-all-start.1 = ((bf16[1,48,4,256]{3,1,0,2:T(8,128)(2,1)}), bf16[1,48,4,256]{3,1,0,2:T(8,128)(2,1)S(1)}, u32[]{:S(2)}, u32[]{:S(2)}) async-start(bf16[1,48,4,256]{3,1,0,2:T(8,128)(2,1)} %copy.22), calls=%async_computation.5 | async-start | bytes 196608 | tf_op jit(solution)/shard_map/all_to_all | solution.py:83
  40.7 25.1 %reduce-scatter.8.cloned.1.call-start = ((), (), s32[]{:S(2)}) async-start(), calls=%async_computation.10 | async-start | bytes 491520 | tf_op jit(solution)/shard_map/reduce_scatter | solution.py:36
  41.9 65.9 %reduce-scatter.16.cloned.1.call-start = ((), (), s32[]{:S(2)}) async-start(), calls=%async_computation.14 | async-start | bytes 983040 | tf_op jit(solution)/shard_map/reduce_scatter | solution.py:36
  65.7 56.6 %reduce-scatter.10.cloned.1.call-start = ((), (), s32[]{:S(2)}) async-start(), calls=%async_computation.11 | async-start | bytes 983040 | tf_op jit(solution)/shard_map/reduce_scatter | solution.py:36
  65.7 1.6 collective-permute-start
  101.6 45.6 %reduce-scatter.12.cloned.1.call-start = ((), (), s32[]{:S(2)}) async-start(), calls=%async_computation.12 | async-start | bytes 983040 | tf_op jit(solution)/shard_map/reduce_scatter | solution.py:36
  107.7 125.6 %reduce-scatter.18.cloned.1.call-start = ((), (), s32[]{:S(2)}) async-start(), calls=%async_computation.15 | async-start | bytes 884736 | tf_op jit(solution)/shard_map/reduce_scatter | solution.py:97
  198.4 80.4 %reduce-scatter.14.cloned.1.call-start = ((), (), s32[]{:S(2)}) async-start(), calls=%async_computation.13 | async-start | bytes 884736 | tf_op jit(solution)/shard_map/reduce_scatter | solution.py:97
  215.2 65.1 %copy-start.1 = (bf16[48,1024]{1,0:T(8,128)(2,1)S(1)}, bf16[48,1024]{1,0:T(8,128)(2,1)}, u32[]{:S(2)}) copy-start(bf16[48,1024]{1,0:T(8,128)(2,1)} %reduce-scatter.8.cloned.1.call-done) | copy-start | bytes 294916
  233.4 8.5 %collective-permute-start.2 = (bf16[48,1024]{1,0:T(8,128)(2,1)}, bf16[48,1024]{1,0:T(8,128)(2,1)S(1)}, u32[]{:S(2)}, u32[]{:S(2)}) collective-permute-start(bf16[48,1024]{1,0:T(8,128)(2,1)} %reduce-scatter.18.cloned.1.call-done), channel_id=1, source_target_pairs={{0,0},{1,1},{2,8},{3,9},{4,16},{5,17},{6,24},{7,25},{8,2},{9,3},{1... | collective-permute-start | bytes 294920 | tf_op jit(solution)/shard_map/ppermute | solution.py:46
  240.1 76.2 %copy-start.2 = (f32[2048]{0:T(1024)S(1)}, f32[2048]{0:T(1024)}, u32[]{:S(2)}) copy-start(f32[2048]{0:T(1024)} %param.10) | copy-start | bytes 24580
  240.1 77.1 %copy-start.3 = (s32[1,128]{1,0:T(1,128)S(1)}, s32[1,128]{1,0:T(1,128)}, u32[]{:S(2)}) copy-start(s32[1,128]{1,0:T(1,128)} %param.9) | copy-start | bytes 1540
  241.8 74.5 %reduce-scatter.20.cloned.1.call-start = ((), (), s32[]{:S(2)}) async-start(), calls=%async_computation.16 | async-start | bytes 294912 | tf_op jit(solution)/shard_map/reduce_scatter | solution.py:122
  278.8 1.5 collective-permute-start.1
Sparse Core Ops, SparseCore 0:
  44.4 21.0 reduce-scatter.7
  67.8 26.4 reduce-scatter.15
  101.7 20.5 reduce-scatter.9
  124.5 22.5 reduce-scatter.11
  198.5 34.8 reduce-scatter.17
  242.0 36.7 reduce-scatter.13
  282.7 33.5 reduce-scatter.19
where the time goes:
time: 327 us; the launch traced here: 326 us
  blocking collectives  131 us (40%)
  waiting for transfers between devices  108 us (33%)
  matrix products  45.5 us (14%)
  between operations  15 us (5%)
  starting transfers between devices  13.1 us (4%)
  local copies, waits for them, and re-layouts  8.58 us (3%)
  other arithmetic  4.91 us (2%)
    reduce_scatter x4, waiting for transfers between devices, grp_total(): lax.psum_scatter(partial_value.astype(bf16), 'grp', scatter_dimension=0,...  39.4 us
    reduce_scatter x1, waiting for transfers between devices, shards(): lax.psum_scatter(term, 'seq', scatter_dimension=0, tiled=True).astype(f32)  35.1 us
    all_gather x1, blocking collectives, spread(): every = lax.all_gather(swap(cols), 'seq', axis=0)  27.1 us
    dot_general x11, matrix products, matmul(): return jnp.dot(a, b, preferred_element_type=f32)  25.2 us
    reduce_scatter x2, waiting for transfers between devices, column_total(): lax.psum_scatter(part, 'seq', scatter_dimension=0, tiled=True)  24.2 us
    dot_general x4, matrix products, matmul_t(): lax.dot_general(a, b, (((1,), (1,)), ((), ())), preferred_element_type=f32)  20.3 us
    all_gather x1, blocking collectives, shards(): grad_gate = lax.all_gather(grad_gate, 'grp', axis=0, tiled=True)  18.2 us
    all_gather x1, blocking collectives, shards(): grad_up = lax.all_gather(grad_up, 'grp', axis=0, tiled=True)  17.4 us
  transfers between devices with their start and end apart: 12, of which 7 were waited for; matrix products, arithmetic and copies ran while one was open for 11% of the time, Pallas kernels for 0%

commit v1 on v0

--- a/solution.py
+++ b/solution.py
@@ -104,8 +104,11 @@
         grad_gate = (grad_hidden * up_value * derivative).astype(bf16)
         grad_up = (grad_hidden * activated).astype(bf16)
         grad_gate = lax.all_gather(grad_gate, "grp", axis=0, tiled=True)
-        grad_up = lax.all_gather(grad_up, "grp", axis=0, tiled=True)
-        hidden = lax.all_gather(hidden, "grp", axis=0, tiled=True)
+        grad_up, hidden = jnp.split(
+            lax.all_gather(jnp.concatenate([grad_up, hidden], axis=1), "grp", axis=0, tiled=True),
+            [grad_up.shape[1]],
+            axis=1,
+        )
         back_cols = column_total(matmul_t(grad_gate, w_gate) + matmul_t(grad_up, w_up))
         down_cols = column_total(matmul(hidden, w_down))
         out_cols = (x_cols.astype(f32) + down_cols).astype(bf16)

time: 327 us -> 329 us (level)
  blocking collectives: 131 us -> 102 us
  waiting for transfers between devices: 108 us -> 136 us
    all_gather x2 -> x0, blocking collectives: 34.2 us -> none  [the longest x1 17.4 us: shards(): grad_up = lax.all_gather(grad_up, 'grp', axis=0, tiled=True)]
    reduce_scatter x2, waiting for transfers between devices: 24.2 us -> 41.5 us  [column_total(): lax.psum_scatter(part, 'seq', scatter_dimension=0, tiled=True)]
    all_gather x0 -> x1, waiting for transfers between devices: none -> 10.3 us  [shards(): lax.all_gather(jnp.concatenate([grad_up, hidden], axis=1), 'grp', axis=0,...]
    all_gather x1, blocking collectives: 18.2 us -> 23.6 us  [shards(): grad_gate = lax.all_gather(grad_gate, 'grp', axis=0, tiled=True)]
  transfers between devices with their start and end apart: 12 -> 13, of which waited for: 7 -> 8; matrix products, arithmetic and copies ran while one was open for 11% -> 13% of each run, Pallas kernels for 0% -> 0%
where the time goes in v1:
time: 329 us; the launch traced here: 328 us
  waiting for transfers between devices  136 us (41%)
  blocking collectives  102 us (31%)
  matrix products  47.5 us (14%)
  between operations  15 us (5%)
  starting transfers between devices  13.1 us (4%)
  local copies, waits for them, and re-layouts  8.59 us (3%)
  other arithmetic  5.77 us (2%)
    reduce_scatter x2, waiting for transfers between devices, column_total(): lax.psum_scatter(part, 'seq', scatter_dimension=0, tiled=True)  41.5 us
    reduce_scatter x4, waiting for transfers between devices, grp_total(): lax.psum_scatter(partial_value.astype(bf16), 'grp', scatter_dimension=0,...  39.4 us
    reduce_scatter x1, waiting for transfers between devices, shards(): lax.psum_scatter(term, 'seq', scatter_dimension=0, tiled=True).astype(f32)  35.1 us
    all_gather x1, blocking collectives, spread(): every = lax.all_gather(swap(cols), 'seq', axis=0)  27.1 us
    dot_general x11, matrix products, matmul(): return jnp.dot(a, b, preferred_element_type=f32)  25.3 us
    all_gather x1, blocking collectives, shards(): grad_gate = lax.all_gather(grad_gate, 'grp', axis=0, tiled=True)  23.6 us
    dot_general x4, matrix products, matmul_t(): lax.dot_general(a, b, (((1,), (1,)), ((), ())), preferred_element_type=f32)  22.2 us
    all_gather x1, blocking collectives, shards(): grad_x = lax.all_gather(grad_x, 'grp', axis=0, tiled=True)  16.1 us
  transfers between devices with their start and end apart: 13, of which 8 were waited for; matrix products, arithmetic and copies ran while one was open for 13% of the time, Pallas kernels for 0%

profile of v1, /device:TPU:0, one launch (start us, length us, event | category | flops | bytes accessed | tf_op | source)
XLA Modules:
  0.0 327.7 jit_solution(10298362406757991626)
XLA Ops:
  7.2 1.4 reduce_max.9
  9.2 1.4 multiply_reduce_fusion.1
  10.6 0.8 multiply_convert_fusion
  11.4 11.3 %all-gather.2 = bf16[8,9,2048]{2,1,0:T(8,128)(2,1)S(1)} all-gather(bf16[1,9,2048]{2,1,0:T(8,128)(2,1)S(1)} %pad_bitcast_fusion), channel_id=2, replica_groups=mesh['grp'=4,'seq'=8] {'seq'}, dimensions={0}, use_global_device_ids=true | all-gather | bytes 331776 | tf_op jit(solution)/shard_map/all_gather | solution.py:61
  22.7 0.2 fusion.41
  22.9 0.1 iota_compare_fusion.1
  23.0 0.2 reduce-window.9
  23.2 0.1 lt.18
  23.3 0.1 iota_add_fusion
  23.4 0.1 add.65
  23.4 0.2 convolution_convert_fusion.6
  23.6 0.1 broadcast_in_dim_reshape.9
  23.8 0.7 copy.18
  24.5 4.9 %all-to-all-start = ((bf16[1,48,4,512]{3,1,0,2:T(8,128)(2,1)}), bf16[1,48,4,512]{3,1,0,2:T(8,128)(2,1)S(1)}, u32[]{:S(2)}, u32[]{:S(2)}) async-start(bf16[1,48,4,512]{3,1,0,2:T(8,128)(2,1)} %copy.18), calls=%async_computation | async-start | bytes 393216 | tf_op jit(solution)/shard_map/all_to_all | solution.py:73
  29.4 1.5 copy.27
  30.9 0.8 dynamic-slice_reduce_fusion
  31.7 0.2 convolution_convert_fusion.10
  31.9 0.1 broadcast_in_dim_reshape.10
  31.9 0.7 copy.20
  32.6 4.8 %all-to-all-done = bf16[1,48,4,512]{3,1,0,2:T(8,128)(2,1)S(1)} async-done(((bf16[1,48,4,512]{3,1,0,2:T(8,128)(2,1)}), bf16[1,48,4,512]{3,1,0,2:T(8,128)(2,1)S(1)}, u32[]{:S(2)}, u32[]{:S(2)}) %all-to-all-start) | async-done | bytes 196640 | tf_op jit(solution)/shard_map/all_to_all | solution.py:73
  37.4 3.3 %all-to-all-start.1 = ((bf16[1,48,4,256]{3,1,0,2:T(8,128)(2,1)}), bf16[1,48,4,256]{3,1,0,2:T(8,128)(2,1)S(1)}, u32[]{:S(2)}, u32[]{:S(2)}) async-start(bf16[1,48,4,256]{3,1,0,2:T(8,128)(2,1)} %copy.20), calls=%async_computation.2 | async-start | bytes 196608 | tf_op jit(solution)/shard_map/all_to_all | solution.py:83
  40.7 0.0 reduce-scatter.8.cloned.1.call-start
  40.7 1.1 convolution_convert_fusion.7
  41.9 0.0 reduce-scatter.10.cloned.1.call-start
  41.9 4.5 %all-to-all-done.1 = bf16[1,48,4,256]{3,1,0,2:T(8,128)(2,1)S(1)} async-done(((bf16[1,48,4,256]{3,1,0,2:T(8,128)(2,1)}), bf16[1,48,4,256]{3,1,0,2:T(8,128)(2,1)S(1)}, u32[]{:S(2)}, u32[]{:S(2)}) %all-to-all-start.1) | async-done | bytes 98336 | tf_op jit(solution)/shard_map/all_to_all | solution.py:83
  46.5 11.9 %all_gather.26 = bf16[192,2048]{1,0:T(8,128)(2,1)S(1)} all-gather(bf16[192,256]{1,0:T(8,128)(2,1)S(1)} %bitcast.91), channel_id=1, replica_groups=mesh['grp'=4,'seq'=8] {'seq'}, dimensions={1}, use_global_device_ids=true | all-gather | bytes 884736 | tf_op jit(solution)/shard_map/all_gather | solution.py:86
  58.4 7.2 %convolution_convert_fusion.3 = bf16[192,2048]{1,0:T(8,128)(2,1)} fusion(bf16[192,2048]{1,0:T(8,128)(2,1)S(1)} %all_gather.26, bf16[2048,2048]{1,0:T(8,128)(2,1)} %param.14), kind=kOutput, calls=%fused_computation.4 | convolution fusion | flops 1611005952 | bytes 9961472 | tf_op jit(solution)/shard_map/dot_general | solution.py:22
  65.7 1.6 collective-permute-start
  67.3 27.1 %all-gather.1 = bf16[384,1024]{1,0:T(8,128)(2,1)S(1)} all-gather(bf16[48,1024]{1,0:T(8,128)(2,1)S(1)} %collective-permute-done), channel_id=3, replica_groups=mesh['grp'=4,'seq'=8] {'seq'}, dimensions={0}, use_global_device_ids=true | all-gather | bytes 884736 | tf_op jit(solution)/shard_map/all_gather | solution.py:90
  94.4 0.8 copy.21
  95.2 0.2 copy.29
  95.5 6.1 %convolution_convert_fusion.2 = bf16[192,2048]{1,0:T(8,128)(2,1)} fusion(bf16[192,2048]{1,0:T(8,128)(2,1)S(1)} %bitcast.85, bf16[2048,2048]{1,0:T(8,128)(2,1)} %param.12), kind=kOutput, calls=%fused_computation.3 | convolution fusion | flops 1611005952 | bytes 9961472 | tf_op jit(solution)/shard_map/dot_general | solution.py:18
  101.6 0.0 reduce-scatter.14.cloned.1.call-start
  101.6 6.1 %convolution_convert_fusion.1 = bf16[192,2048]{1,0:T(8,128)(2,1)} fusion(bf16[192,2048]{1,0:T(8,128)(2,1)S(1)} %bitcast.86, bf16[2048,2048]{1,0:T(8,128)(2,1)} %param.13), kind=kOutput, calls=%fused_computation.2 | convolution fusion | flops 1611005952 | bytes 9961472 | tf_op jit(solution)/shard_map/dot_general | solution.py:18
  107.7 0.0 all-gather.5.cloned.1.call-start
  107.8 14.5 %reduce-scatter.12.cloned.1.call-done = bf16[48,2048]{1,0:T(8,128)(2,1)} async-done(((bf16[192,2048]{1,0:T(8,128)(2,1)}), bf16[48,2048]{1,0:T(8,128)(2,1)}) %reduce-scatter.12.cloned.1.call-update) | async-done | bytes 196624 | tf_op jit(solution)/shard_map/reduce_scatter | solution.py:36
  122.3 24.9 %reduce-scatter.14.cloned.1.call-done = bf16[48,2048]{1,0:T(8,128)(2,1)} async-done(((bf16[192,2048]{1,0:T(8,128)(2,1)}), bf16[48,2048]{1,0:T(8,128)(2,1)}) %reduce-scatter.14.cloned.1.call-update) | async-done | bytes 196624 | tf_op jit(solution)/shard_map/reduce_scatter | solution.py:36
  147.2 1.4 fusion.10
  148.5 0.8 pad_maximum_fusion
  149.3 0.0 reduce-scatter.18.cloned.1.call-start
  149.4 23.6 %all_gather.30 = bf16[192,2048]{1,0:T(8,128)(2,1)S(1)} all-gather(bf16[48,2048]{1,0:T(8,128)(2,1)S(1)} %get-tuple-element.2), channel_id=1, replica_groups=mesh['grp'=4,'seq'=8] {'grp'}, dimensions={0}, use_global_device_ids=true | all-gather | bytes 983040 | tf_op jit(solution)/shard_map/all_gather | solution.py:106
  172.9 7.5 %fusion.45 = f32[192,2048]{1,0:T(8,128)} fusion(bf16[192,2048]{1,0:T(8,128)(2,1)S(1)} %all_gather.30, bf16[2048,2048]{1,0:T(8,128)(2,1)} %param.12), kind=kOutput, calls=%fused_computation.76 | convolution fusion | flops 1610612736 | bytes 10747904 | tf_op jit(solution)/shard_map/dot_general | solution.py:22
  180.4 10.3 %all-gather.5.cloned.1.call-done = bf16[192,4096]{1,0:T(8,128)(2,1)} async-done(((bf16[48,4096]{1,0:T(8,128)(2,1)}), bf16[192,4096]{1,0:T(8,128)(2,1)}) %all-gather.5.cloned.1.call-update) | async-done | bytes 1572880 | tf_op jit(solution)/shard_map/all_gather | solution.py:108
  190.7 6.9 %fusion = bf16[192,2048]{1,0:T(8,128)(2,1)S(1)} fusion(f32[192,2048]{1,0:T(8,128)} %fusion.45, bf16[2048,2048]{1,0:T(8,128)(2,1)} %param.13, bf16[192,4096]{1,0:T(8,128)(2,1)} %all-gather.5.cloned.1.call-done), kind=kOutput, calls=%fused_computation.5 | convolution fusion | flops 1611399168 | bytes 11534336 | tf_op jit(solution)/shard_map/dot_general | solution.py:22
  197.7 0.6 reshape.115
  198.2 1.1 copy.23
  199.4 35.4 %reduce-scatter.18.cloned.1.call-done = bf16[48,1024]{1,0:T(8,128)(2,1)} async-done(((bf16[384,1024]{1,0:T(8,128)(2,1)}), bf16[48,1024]{1,0:T(8,128)(2,1)}) %reduce-scatter.18.cloned.1.call-update) | async-done | bytes 98320 | tf_op jit(solution)/shard_map/reduce_scatter | solution.py:97
  234.8 1.5 collective-permute-start.2
  236.4 5.4 %convolution_convert_fusion = bf16[192,2048]{1,0:T(8,128)(2,1)S(1)} fusion(bf16[2048,2048]{1,0:T(8,128)(2,1)} %param.14, bf16[192,4096]{1,0:T(8,128)(2,1)} %all-gather.5.cloned.1.call-done), kind=kOutput, calls=%fused_computation.1 | convolution fusion | flops 1611005952 | bytes 9961472 | tf_op jit(solution)/shard_map/dot_general | solution.py:18
  241.8 0.6 reshape.113
  242.4 1.1 copy.22
  243.5 0.0 reduce-scatter.20.cloned.1.call-start
  243.6 1.1 add_convert_fusion
  244.7 16.1 %all_gather.31 = bf16[192,1024]{1,0:T(8,128)(2,1)S(1)} all-gather(bf16[48,1024]{1,0:T(8,128)(2,1)S(1)} %add_convert_fusion), channel_id=1, replica_groups=mesh['grp'=4,'seq'=8] {'grp'}, dimensions={0}, use_global_device_ids=true | all-gather | bytes 491520 | tf_op jit(solution)/shard_map/all_gather | solution.py:119
  260.8 0.5 convolution_convert_fusion.8
  261.3 11.9 %all_to_all.45 = bf16[4,48,1,512]{3,1,2,0:T(8,128)(2,1)S(1)} all-to-all(bf16[4,48,1,512]{3,1,2,0:T(8,128)(2,1)S(1)} %bitcast.83), channel_id=1, replica_groups=mesh['grp'=4,'seq'=8] {'grp'}, dimensions={0} | all-to-all | bytes 393216 | tf_op jit(solution)/shard_map/all_to_all | solution.py:121
  273.2 0.2 copy.25
  273.4 1.0 convolution_convert_fusion.5
  274.4 6.1 %reduce-scatter.16.cloned.1.call-done = bf16[48,1024]{1,0:T(8,128)(2,1)} async-done(((bf16[384,1024]{1,0:T(8,128)(2,1)}), bf16[48,1024]{1,0:T(8,128)(2,1)}) %reduce-scatter.16.cloned.1.call-update) | async-done | bytes 98320 | tf_op jit(solution)/shard_map/reduce_scatter | solution.py:97
  280.5 1.5 collective-permute-start.1
  282.0 0.9 fusion.2
  282.9 35.1 %reduce-scatter.20.cloned.1.call-done = bf16[8,2048]{1,0:T(8,128)(2,1)} async-done(((bf16[64,2048]{1,0:T(8,128)(2,1)}), bf16[8,2048]{1,0:T(8,128)(2,1)}) %reduce-scatter.20.cloned.1.call-update) | async-done | bytes 32784 | tf_op jit(solution)/shard_map/reduce_scatter | solution.py:125
  318.0 0.9 multiply_reduce_fusion
  318.9 1.9 fusion.1
  (29 shorter events, 0.4 us)
Async XLA Ops:
  7.2 33.6 %copy-start = (bf16[512,1024]{1,0:T(8,128)(2,1)S(1)}, bf16[512,1024]{1,0:T(8,128)(2,1)}, u32[]{:S(2)}) copy-start(bf16[512,1024]{1,0:T(8,128)(2,1)} %param.11) | copy-start | bytes 3145732
  24.5 12.9 %all-to-all-start = ((bf16[1,48,4,512]{3,1,0,2:T(8,128)(2,1)}), bf16[1,48,4,512]{3,1,0,2:T(8,128)(2,1)S(1)}, u32[]{:S(2)}, u32[]{:S(2)}) async-start(bf16[1,48,4,512]{3,1,0,2:T(8,128)(2,1)} %copy.18), calls=%async_computation | async-start | bytes 393216 | tf_op jit(solution)/shard_map/all_to_all | solution.py:73
  37.4 9.1 %all-to-all-start.1 = ((bf16[1,48,4,256]{3,1,0,2:T(8,128)(2,1)}), bf16[1,48,4,256]{3,1,0,2:T(8,128)(2,1)S(1)}, u32[]{:S(2)}, u32[]{:S(2)}) async-start(bf16[1,48,4,256]{3,1,0,2:T(8,128)(2,1)} %copy.20), calls=%async_computation.2 | async-start | bytes 196608 | tf_op jit(solution)/shard_map/all_to_all | solution.py:83
  40.7 25.1 %reduce-scatter.8.cloned.1.call-start = ((), (), s32[]{:S(2)}) async-start(), calls=%async_computation.10 | async-start | bytes 491520 | tf_op jit(solution)/shard_map/reduce_scatter | solution.py:36
  41.9 65.9 %reduce-scatter.10.cloned.1.call-start = ((), (), s32[]{:S(2)}) async-start(), calls=%async_computation.11 | async-start | bytes 983040 | tf_op jit(solution)/shard_map/reduce_scatter | solution.py:36
  65.7 56.6 %reduce-scatter.12.cloned.1.call-start = ((), (), s32[]{:S(2)}) async-start(), calls=%async_computation.12 | async-start | bytes 983040 | tf_op jit(solution)/shard_map/reduce_scatter | solution.py:36
  65.7 1.6 collective-permute-start
  101.6 45.6 %reduce-scatter.14.cloned.1.call-start = ((), (), s32[]{:S(2)}) async-start(), calls=%async_computation.13 | async-start | bytes 983040 | tf_op jit(solution)/shard_map/reduce_scatter | solution.py:36
  107.7 83.0 %all-gather.5.cloned.1.call-start = ((), (), s32[]{:S(2)}) async-start(), calls=%async_computation.14 | async-start | bytes 1966080 | tf_op jit(solution)/shard_map/all_gather | solution.py:108
  149.3 85.5 %reduce-scatter.18.cloned.1.call-start = ((), (), s32[]{:S(2)}) async-start(), calls=%async_computation.16 | async-start | bytes 884736 | tf_op jit(solution)/shard_map/reduce_scatter | solution.py:97
  199.4 82.7 %copy-start.1 = (bf16[48,1024]{1,0:T(8,128)(2,1)S(1)}, bf16[48,1024]{1,0:T(8,128)(2,1)}, u32[]{:S(2)}) copy-start(bf16[48,1024]{1,0:T(8,128)(2,1)} %reduce-scatter.8.cloned.1.call-done) | copy-start | bytes 294916
  199.4 81.1 %reduce-scatter.16.cloned.1.call-start = ((), (), s32[]{:S(2)}) async-start(), calls=%async_computation.15 | async-start | bytes 884736 | tf_op jit(solution)/shard_map/reduce_scatter | solution.py:97
  234.8 8.8 %collective-permute-start.2 = (bf16[48,1024]{1,0:T(8,128)(2,1)}, bf16[48,1024]{1,0:T(8,128)(2,1)S(1)}, u32[]{:S(2)}, u32[]{:S(2)}) collective-permute-start(bf16[48,1024]{1,0:T(8,128)(2,1)} %reduce-scatter.18.cloned.1.call-done), channel_id=1, source_target_pairs={{0,0},{1,1},{2,8},{3,9},{4,16},{5,17},{6,24},{7,25},{8,2},{9,3},{1... | collective-permute-start | bytes 294920 | tf_op jit(solution)/shard_map/ppermute | solution.py:46
  241.8 76.2 %copy-start.2 = (f32[2048]{0:T(1024)S(1)}, f32[2048]{0:T(1024)}, u32[]{:S(2)}) copy-start(f32[2048]{0:T(1024)} %param.10) | copy-start | bytes 24580
  241.8 77.1 %copy-start.3 = (s32[1,128]{1,0:T(1,128)S(1)}, s32[1,128]{1,0:T(1,128)}, u32[]{:S(2)}) copy-start(s32[1,128]{1,0:T(1,128)} %param.9) | copy-start | bytes 1540
  243.5 74.5 %reduce-scatter.20.cloned.1.call-start = ((), (), s32[]{:S(2)}) async-start(), calls=%async_computation.17 | async-start | bytes 294912 | tf_op jit(solution)/shard_map/reduce_scatter | solution.py:125
  280.5 1.5 collective-permute-start.1
Sparse Core Ops, SparseCore 0:
  44.4 21.0 reduce-scatter.7
  67.8 26.4 reduce-scatter.9
  101.7 20.5 reduce-scatter.11
  124.6 22.5 reduce-scatter.13
  149.4 41.2 all-gather.4
  199.5 35.3 reduce-scatter.17
  243.7 36.7 reduce-scatter.15
  284.4 33.5 reduce-scatter.19
